TPU v7x, 128 devices: a whole 4x4x4 slice. The times are simulated.
128 devices in a mesh: room: 4 (over x_hi, core), geom: 32 (over z, x_lo, y).
Axes of the slice: x: 4 (x_hi: 2, x_lo: 2; x = x_hi * 2 + x_lo), y: 4, z: 4, core: 2. Of those that a mesh axis runs over, the one named last changes fastest.
Arguments:
- queries: bfloat16 [4, 4096, 512], P('room', 'geom'), may hold values from -6 to 6
- features: bfloat16 [4, 4096, 512], P('room', 'geom'), may hold values from -45 to 45
- visible: int32 [4, 32, 32], P('room', 'geom'), may hold values from 0 to 1, as said below
- cotangent: bfloat16 [4, 4096, 512], P('room', 'geom'), may hold values from -0.125 to 0.125
- w_query: bfloat16 [512, 512], replicated, may hold values from -0.25 to 0.25
- w_key: bfloat16 [512, 512], replicated, may hold values from -0.25 to 0.25
- w_value: bfloat16 [512, 512], replicated, may hold values from -0.25 to 0.25
- w_out: bfloat16 [512, 512], replicated, may hold values from -0.25 to 0.25
- w_up: bfloat16 [512, 1024], replicated, may hold values from -0.25 to 0.25
- w_down: bfloat16 [1024, 512], replicated, may hold values from -0.1875 to 0.1875
- gain_attn: float32 [512], replicated, may hold values from 0.25 to 1.75
- gain_mlp: float32 [512], replicated, may hold values from 0.25 to 1.75
Outputs:
- output: bfloat16 [4, 4096, 512], P('room', 'geom')
- grad_query_w: bfloat16 [512, 512], replicated
- grad_key_w: bfloat16 [512, 512], replicated
- grad_value_w: bfloat16 [512, 512], replicated
- grad_out_w: bfloat16 [512, 512], replicated
- grad_up_w: bfloat16 [512, 1024], replicated
- grad_down_w: bfloat16 [1024, 512], replicated
- grad_gain_attn: bfloat16 [512], replicated
- grad_gain_mlp: bfloat16 [512], replicated
Inputs may be any that keep to these rules, and one draw needn't show every extreme that they name: `visible`: every query block sees at least one key block.
All inputs are finite; a program needn't handle non-finite values.
Results may differ from a plain program's by a relative error of at most 0.017.
The roundings to bfloat16 on the way count: a program that leaves them out, or rounds other values in their place, can miss the bound.
Values may be sent and summed in bfloat16 or wider, within the bound.
No kernel may reach another device: no remote copies, remote signals or barrier semaphores. Data moves between devices by JAX's collectives and lax.ppermute only.
A program may use at most 128 MiB of HBM per device.

v0:
```python
import math
import jax
import jax.numpy as jnp
from jax import lax
from jax.sharding import PartitionSpec as P

HEADS = 4
BLK = 128
EPSILON = 1e-05
GELU_COEF = math.sqrt(2.0 / math.pi)


def normalize(inputs, gain):
    center = inputs - jnp.mean(inputs, axis=-1, keepdims=True)
    inverse = lax.rsqrt(jnp.mean(center * center, axis=-1, keepdims=True) + EPSILON)
    scaled = center * inverse
    return (scaled, inverse, scaled * gain)


def gelu_pair(inputs):
    inner = GELU_COEF * (inputs + 0.044715 * inputs * inputs * inputs)
    tangent = jnp.tanh(inner)
    value = 0.5 * inputs * (1.0 + tangent)
    slope = 0.5 * (1.0 + tangent) + 0.5 * inputs * (1.0 - tangent * tangent) * GELU_COEF * (
        1.0 + 3.0 * 0.044715 * inputs * inputs
    )
    return (value, slope)


def mult_nt(left, right):
    return lax.dot_general(
        left, right, (((1,), (1,)), ((), ())), preferred_element_type=jnp.float32
    )


def mult_tn(left, right):
    return lax.dot_general(
        left, right, (((0,), (0,)), ((), ())), preferred_element_type=jnp.float32
    )


def device_step(
    queries,
    visible,
    cotangent,
    key_rows,
    value_rows,
    w_query,
    w_out,
    w_up,
    w_down,
    gain_attn,
    gain_mlp,
):
    head_size = key_rows.shape[1] // HEADS
    factor = 1.0 / math.sqrt(head_size)
    allowed = jnp.repeat(jnp.repeat(visible > 0, BLK, axis=0), BLK, axis=1)
    inputs = queries.astype(jnp.float32)
    scaled_one, inverse_one, normed = normalize(inputs, gain_attn)
    normed_b = normed.astype(jnp.bfloat16)
    query_rows = jnp.dot(normed_b, w_query, preferred_element_type=jnp.float32).astype(jnp.bfloat16)
    contexts = []
    saved = []
    for head_index in range(HEADS):
        lower = head_index * head_size
        query_head = query_rows[:, lower : lower + head_size]
        key_head = key_rows[:, lower : lower + head_size]
        value_head = value_rows[:, lower : lower + head_size]
        scores = mult_nt(query_head, key_head) * factor
        scores = jnp.where(allowed, scores, -1e30)
        highest = jnp.max(scores, axis=-1, keepdims=True)
        expo = jnp.exp(scores - highest)
        attend = expo / jnp.sum(expo, axis=-1, keepdims=True)
        attend_b = attend.astype(jnp.bfloat16)
        contexts.append(
            jnp.dot(attend_b, value_head, preferred_element_type=jnp.float32).astype(jnp.bfloat16)
        )
        saved.append((attend, attend_b))
    context = jnp.concatenate(contexts, axis=1)
    mixed = inputs + jnp.dot(context, w_out, preferred_element_type=jnp.float32)
    scaled_two, inverse_two, normed_two = normalize(mixed, gain_mlp)
    normed_two_b = normed_two.astype(jnp.bfloat16)
    upper = jnp.dot(normed_two_b, w_up, preferred_element_type=jnp.float32)
    activated, slope = gelu_pair(upper)
    activated_b = activated.astype(jnp.bfloat16)
    output = (mixed + jnp.dot(activated_b, w_down, preferred_element_type=jnp.float32)).astype(
        jnp.bfloat16
    )
    grad_down = mult_tn(activated_b, cotangent)
    grad_activated = mult_nt(cotangent, w_down)
    grad_upper_b = (grad_activated * slope).astype(jnp.bfloat16)
    grad_up = mult_tn(normed_two_b, grad_upper_b)
    grad_normed_two = mult_nt(grad_upper_b, w_up)
    grad_gain_mlp = jnp.sum(grad_normed_two * scaled_two, axis=0)
    grad_scaled = grad_normed_two * gain_mlp
    mean_one = jnp.mean(grad_scaled, axis=-1, keepdims=True)
    mean_two = jnp.mean(grad_scaled * scaled_two, axis=-1, keepdims=True)
    grad_mixed = cotangent.astype(jnp.float32) + inverse_two * (
        grad_scaled - mean_one - scaled_two * mean_two
    )
    grad_mixed_b = grad_mixed.astype(jnp.bfloat16)
    grad_out = mult_tn(context, grad_mixed_b)
    grad_context = mult_nt(grad_mixed_b, w_out).astype(jnp.bfloat16)
    grad_queries = []
    grad_keys = []
    grad_values = []
    for head_index in range(HEADS):
        lower = head_index * head_size
        query_head = query_rows[:, lower : lower + head_size]
        key_head = key_rows[:, lower : lower + head_size]
        value_head = value_rows[:, lower : lower + head_size]
        attend, attend_b = saved[head_index]
        grad_head = grad_context[:, lower : lower + head_size]
        grad_attend = mult_nt(grad_head, value_head)
        grad_values.append(mult_tn(attend_b, grad_head))
        centre = jnp.sum(attend * grad_attend, axis=-1, keepdims=True)
        grad_scores = (attend * (grad_attend - centre) * factor).astype(jnp.bfloat16)
        grad_queries.append(jnp.dot(grad_scores, key_head, preferred_element_type=jnp.float32))
        grad_keys.append(mult_tn(grad_scores, query_head))
    grad_query_rows = jnp.concatenate(grad_queries, axis=1).astype(jnp.bfloat16)
    partial_keys = jnp.concatenate(grad_keys, axis=1).astype(jnp.bfloat16)
    partial_values = jnp.concatenate(grad_values, axis=1).astype(jnp.bfloat16)
    grad_query = mult_tn(normed_b, grad_query_rows)
    grad_normed = mult_nt(grad_query_rows, w_query)
    grad_gain_attn = jnp.sum(grad_normed * scaled_one, axis=0)
    grads = (grad_query, grad_out, grad_up, grad_down, grad_gain_attn, grad_gain_mlp)
    return (output, grads, partial_keys, partial_values)


def local(
    queries,
    features,
    visible,
    cotangent,
    w_query,
    w_key,
    w_value,
    w_out,
    w_up,
    w_down,
    gain_attn,
    gain_mlp,
):
    local_feat = features[0]
    local_keys = jnp.dot(local_feat, w_key, preferred_element_type=jnp.float32).astype(jnp.bfloat16)
    local_values = jnp.dot(local_feat, w_value, preferred_element_type=jnp.float32).astype(
        jnp.bfloat16
    )
    key_rows, value_rows = (
        lax.all_gather(local_keys, "geom", axis=0, tiled=True),
        lax.all_gather(local_values, "geom", axis=0, tiled=True),
    )
    output, grads, partial_keys, partial_values = device_step(
        queries[0],
        visible[0],
        cotangent[0],
        key_rows,
        value_rows,
        w_query,
        w_out,
        w_up,
        w_down,
        gain_attn,
        gain_mlp,
    )
    key_sum, value_sum = (
        lax.psum_scatter(partial_keys.astype(jnp.float32), "geom", scatter_dimension=0, tiled=True),
        lax.psum_scatter(
            partial_values.astype(jnp.float32), "geom", scatter_dimension=0, tiled=True
        ),
    )
    feat_float = local_feat.astype(jnp.float32)
    grad_key = lax.dot_general(
        feat_float,
        key_sum,
        (((0,), (0,)), ((), ())),
        precision=lax.Precision.HIGHEST,
        preferred_element_type=jnp.float32,
    )
    grad_value = lax.dot_general(
        feat_float,
        value_sum,
        (((0,), (0,)), ((), ())),
        precision=lax.Precision.HIGHEST,
        preferred_element_type=jnp.float32,
    )
    grad_query, grad_out, grad_up, grad_down, grad_gain_attn, grad_gain_mlp = grads
    totals = lax.psum(
        (
            grad_query,
            grad_key,
            grad_value,
            grad_out,
            grad_up,
            grad_down,
            grad_gain_attn,
            grad_gain_mlp,
        ),
        ("room", "geom"),
    )
    summed = [piece.astype(jnp.bfloat16) for piece in totals]
    return (
        output[None],
        summed[0],
        summed[1],
        summed[2],
        summed[3],
        summed[4],
        summed[5],
        summed[6],
        summed[7],
    )


def solution(mesh):
    placed = (
        P("room", "geom", None),
        P("room", "geom", None),
        P("room", "geom", None),
        P("room", "geom", None),
        P(),
        P(),
        P(),
        P(),
        P(),
        P(),
        P(),
        P(),
    )
    return jax.shard_map(
        local,
        mesh=mesh,
        in_specs=placed,
        out_specs=(P("room", "geom", None), P(), P(), P(), P(), P(), P(), P(), P()),
        check_vma=False,
    )
```

profile of v0, /device:TPU:0, one launch (start us, length us, event | category | flops | bytes accessed | tf_op | source)
XLA Modules:
  0.0 832.1 jit_solution(216690923784676051)
XLA Ops:
  7.3 2.1 convolution_convert_fusion.10
  9.5 2.0 convolution_convert_fusion.9
  14.1 156.3 %all-gather.3.cloned.1.call-done = bf16[4096,512]{1,0:T(8,128)(2,1)} async-done(((bf16[128,512]{1,0:T(8,128)(2,1)}), bf16[4096,512]{1,0:T(8,128)(2,1)}) %all-gather.3.cloned.1.call-update) | async-done | bytes 4194320 | tf_op jit(solution)/shard_map/all_gather | solution.py:150
  170.4 1.9 fusion.99
  172.3 1.4 copy-done.8
  174.7 1.3 copy-done.5
  178.8 151.2 %all-gather.5.cloned.1.call-done = bf16[4096,512]{1,0:T(8,128)(2,1)} async-done(((bf16[128,512]{1,0:T(8,128)(2,1)}), bf16[4096,512]{1,0:T(8,128)(2,1)}) %all-gather.5.cloned.1.call-update) | async-done | bytes 4194320 | tf_op jit(solution)/shard_map/all_gather | solution.py:151
  329.9 2.7 convolution_convert_fusion.19
  344.3 3.6 maximum_convert_fusion.1
  348.6 2.7 multiply_reduce_fusion.3
  356.4 1.5 copy-done.4
  362.9 3.9 maximum_convert_fusion
  366.8 1.9 convolution_convert_fusion.15
  368.8 2.1 convolution_convert_fusion.14
  373.6 1.3 fusion.79
  374.9 1.4 fusion.78
  376.3 1.9 fusion.55
  379.2 147.8 %reduce-scatter.5.cloned.1.call-done = f32[128,512]{1,0:T(8,128)} async-done(((f32[4096,512]{1,0:T(8,128)}), f32[128,512]{1,0:T(8,128)}) %reduce-scatter.5.cloned.1.call-update) | async-done | bytes 262160 | tf_op jit(solution)/shard_map/reduce_scatter | solution.py:168
  526.9 2.5 convolution_bitcast_fusion
  529.5 174.9 %reduce-scatter.3.cloned.1.call-done = f32[128,512]{1,0:T(8,128)} async-done(((f32[4096,512]{1,0:T(8,128)}), f32[128,512]{1,0:T(8,128)}) %reduce-scatter.3.cloned.1.call-update) | async-done | bytes 262160 | tf_op jit(solution)/shard_map/reduce_scatter | solution.py:167
  704.4 2.6 convolution_bitcast_fusion.1
  707.0 114.5 %all-reduce.2 = (bf16[512,512]{1,0:T(8,128)(2,1)}, bf16[512,512]{0,1:T(8,128)(2,1)}, bf16[512,512]{0,1:T(8,128)(2,1)}, bf16[512,512]{1,0:T(8,128)(2,1)}, bf16[51...) all-reduce(f32[512,512]{1,0:T(8,128)} %fusion.78, ...), channel_id=1, replica_groups=mesh['room'=4,'geom'=32] {'room','geom'}, use_global_device_ids=true, to_apply=%region_18.19 | all-reduce | flops 2098176 | bytes 12589056 | tf_op jit(solution)/shard_map/psum | solution.py:188
  821.4 2.0 copy.21
  823.5 2.0 copy.22
  (218 shorter events, 32.0 us)
Async XLA Ops:
  7.2 330.5 %copy-start = (bf16[512,1024]{1,0:T(8,128)(2,1)S(1)}, bf16[512,1024]{1,0:T(8,128)(2,1)}, u32[]{:S(2)}) copy-start(bf16[512,1024]{1,0:T(8,128)(2,1)} %param.20) | copy-start | bytes 3145732
  7.2 6.6 copy-start.19
  7.2 6.5 copy-start.82
  7.2 6.6 copy-start.30
  7.2 6.6 copy-start.45
  7.2 163.2 %all-gather.3.cloned.1.call-start = ((), (), s32[]{:S(2)}) async-start(), calls=%async_computation.2 | async-start | bytes 4325376 | tf_op jit(solution)/shard_map/all_gather | solution.py:150
  9.4 320.5 %all-gather.5.cloned.1.call-start = ((), (), s32[]{:S(2)}) async-start(), calls=%async_computation.3 | async-start | bytes 4325376 | tf_op jit(solution)/shard_map/all_gather | solution.py:151
  11.5 515.4 %reduce-scatter.5.cloned.1.call-start = ((), (), s32[]{:S(2)}) async-start(), calls=%async_computation.5 | async-start | bytes 8650752 | tf_op jit(solution)/shard_map/reduce_scatter | solution.py:168
  12.6 161.6 %copy-start.47 = (f32[128]{0:T(128)}, f32[128]{0:T(128)S(1)}, u32[]{:S(2)}) copy-start(f32[128]{0:T(128)S(1)} %broadcast_multiply_fusion.3) | copy-start | bytes 1540
  13.7 160.4 %copy-start.62 = (f32[128]{0:T(128)}, f32[128]{0:T(128)S(1)}, u32[]{:S(2)}) copy-start(f32[128]{0:T(128)S(1)} %add_rsqrt_fusion.1) | copy-start | bytes 1540
  14.1 163.4 %copy-start.24 = (bf16[128,512]{1,0:T(8,128)(2,1)}, bf16[128,512]{1,0:T(8,128)(2,1)S(1)}, u32[]{:S(2)}) copy-start(bf16[128,512]{1,0:T(8,128)(2,1)S(1)} %convolution_convert_fusion.11) | copy-start | bytes 393220
  172.3 157.6 %copy-start.58 = (f32[128]{0:T(128)}, f32[128]{0:T(128)S(1)}, u32[]{:S(2)}) copy-start(f32[128]{0:T(128)S(1)} %get-tuple-element.35) | copy-start | bytes 1540
  174.1 155.8 %copy-start.73 = (f32[128]{0:T(128)}, f32[128]{0:T(128)S(1)}, u32[]{:S(2)}) copy-start(f32[128]{0:T(128)S(1)} %fusion.5) | copy-start | bytes 1540
  174.7 157.9 %copy-start.55 = (f32[128]{0:T(128)}, f32[128]{0:T(128)S(1)}, u32[]{:S(2)}) copy-start(f32[128]{0:T(128)S(1)} %get-tuple-element.33) | copy-start | bytes 1540
  176.4 156.2 %copy-start.70 = (f32[128]{0:T(128)}, f32[128]{0:T(128)S(1)}, u32[]{:S(2)}) copy-start(f32[128]{0:T(128)S(1)} %fusion.7) | copy-start | bytes 1540
  177.0 157.5 %copy-start.52 = (f32[128]{0:T(128)}, f32[128]{0:T(128)S(1)}, u32[]{:S(2)}) copy-start(f32[128]{0:T(128)S(1)} %get-tuple-element.31) | copy-start | bytes 1540
  177.5 157.0 %copy-start.67 = (f32[128]{0:T(128)}, f32[128]{0:T(128)S(1)}, u32[]{:S(2)}) copy-start(f32[128]{0:T(128)S(1)} %fusion.9) | copy-start | bytes 1540
  178.3 157.7 %copy-start.49 = (f32[128]{0:T(128)}, f32[128]{0:T(128)S(1)}, u32[]{:S(2)}) copy-start(f32[128]{0:T(128)S(1)} %get-tuple-element.29) | copy-start | bytes 1540
  178.7 157.3 %copy-start.64 = (f32[128]{0:T(128)}, f32[128]{0:T(128)S(1)}, u32[]{:S(2)}) copy-start(f32[128]{0:T(128)S(1)} %fusion.11) | copy-start | bytes 1540
  347.9 356.5 %reduce-scatter.3.cloned.1.call-start = ((), (), s32[]{:S(2)}) async-start(), calls=%async_computation.4 | async-start | bytes 8650752 | tf_op jit(solution)/shard_map/reduce_scatter | solution.py:167
  376.3 150.7 %copy-start.23 = (bf16[1,128,512]{2,1,0:T(8,128)(2,1)S(1)}, bf16[1,128,512]{2,1,0:T(8,128)(2,1)}, u32[]{:S(2)}) copy-start(bf16[1,128,512]{2,1,0:T(8,128)(2,1)} %param.13) | copy-start | bytes 393220
  378.1 328.8 %copy-start.46 = (f32[512]{0:T(512)S(1)}, f32[512]{0:T(512)}, u32[]{:S(2)}) copy-start(f32[512]{0:T(512)} %get-tuple-element.18) | copy-start | bytes 6148
  378.1 328.8 %copy-start.77 = (f32[512]{0:T(512)S(1)}, f32[512]{0:T(512)}, u32[]{:S(2)}) copy-start(f32[512]{0:T(512)} %fusion.14) | copy-start | bytes 6148
  707.0 118.6 %copy-start.1 = (bf16[512,1024]{1,0:T(8,128)(2,1)S(1)}, bf16[512,1024]{1,0:T(8,128)(2,1)}, u32[]{:S(2)}) copy-start(bf16[512,1024]{1,0:T(8,128)(2,1)} %param.20) | copy-start | bytes 3145732
  (63 other events, 114.5 us)
Sparse Core Ops, SparseCore 0:
  10.3 160.0 all-gather.2
  172.6 157.2 all-gather.4
  348.0 178.8 reduce-scatter.4
  529.2 175.1 reduce-scatter.2
where the time goes:
time: 833 us; the launch traced here: 832 us
  waiting for transfers between devices  630 us (76%)
  blocking collectives  114 us (14%)
  matrix products  41.7 us (5%)
  local copies, waits for them, and re-layouts  16 us (2%)
  between operations  14.7 us (2%)
  other arithmetic  14.5 us (2%)
    reduce_scatter x1, waiting for transfers between devices, local(): lax.psum_scatter(partial_keys.astype(jnp.float32), 'geom', scatter_dimens...  175 us
    all_gather x1, waiting for transfers between devices, local(): lax.all_gather(local_keys, 'geom', axis=0, tiled=True)  156 us
    all_gather x1, waiting for transfers between devices, local(): lax.all_gather(local_values, 'geom', axis=0, tiled=True)  151 us
    reduce_scatter x1, waiting for transfers between devices, local(): lax.psum_scatter(partial_values.astype(jnp.float32), 'geom', scatter_dime...  148 us
    psum x1, blocking collectives, local(): lax.psum((grad_query, grad_key, grad_value, grad_out, grad_up, grad_down,...  114 us
  transfers between devices with their start and end apart: 4, of which 4 were waited for; matrix products, arithmetic and copies ran while one was open for 5% of the time, Pallas kernels for 0%

commit v1 on v0

--- a/solution.py
+++ b/solution.py
@@ -3,11 +3,18 @@
 import jax.numpy as jnp
 from jax import lax
 from jax.sharding import PartitionSpec as P
+from jax.lax import psum
 
 HEADS = 4
 BLK = 128
 EPSILON = 1e-05
 GELU_COEF = math.sqrt(2.0 / math.pi)
+
+
+def _convert_levels_all(row_data, axis_id, shard_axis):
+    for c in (axis_id, shard_axis):
+        row_data = psum(row_data, c)
+    return row_data
 
 
 def normalize(inputs, gain):
@@ -185,7 +192,7 @@
         preferred_element_type=jnp.float32,
     )
     grad_query, grad_out, grad_up, grad_down, grad_gain_attn, grad_gain_mlp = grads
-    totals = lax.psum(
+    totals = _convert_levels_all(
         (
             grad_query,
             grad_key,
@@ -196,7 +203,8 @@
             grad_gain_attn,
             grad_gain_mlp,
         ),
-        ("room", "geom"),
+        "geom",
+        "room",
     )
     summed = [piece.astype(jnp.bfloat16) for piece in totals]
     return (

time: 833 us -> 1210 us (1.45)
  waiting for transfers between devices: 630 us -> 889 us
  blocking collectives: 114 us -> 227 us
    psum x0 -> x1, waiting for transfers between devices: none -> 259 us  [_convert_levels_all(): row_data = psum(row_data, c)]
    psum x1 -> x2, blocking collectives: 114 us -> 227 us  [_convert_levels_all(): row_data = psum(row_data, c)]
  transfers between devices with their start and end apart: 4 -> 5, of which waited for: 4 -> 5; matrix products, arithmetic and copies ran while one was open for 5% -> 3% of each run, Pallas kernels for 0% -> 0%
where the time goes in v1:
time: 1210 us; the launch traced here: 1200 us
  waiting for transfers between devices  889 us (73%)
  blocking collectives  227 us (19%)
  matrix products  44.1 us (4%)
  local copies, waits for them, and re-layouts  15 us (1%)
  between operations  14.7 us (1%)
  other arithmetic  14.3 us (1%)
    psum x1, waiting for transfers between devices, _convert_levels_all(): row_data = psum(row_data, c)  259 us
    psum x2, blocking collectives, _convert_levels_all(): row_data = psum(row_data, c)  227 us
    reduce_scatter x1, waiting for transfers between devices, local(): lax.psum_scatter(partial_keys.astype(jnp.float32), 'geom', scatter_dimens...  175 us
    all_gather x1, waiting for transfers between devices, local(): lax.all_gather(local_keys, 'geom', axis=0, tiled=True)  156 us
    all_gather x1, waiting for transfers between devices, local(): lax.all_gather(local_values, 'geom', axis=0, tiled=True)  151 us
    reduce_scatter x1, waiting for transfers between devices, local(): lax.psum_scatter(partial_values.astype(jnp.float32), 'geom', scatter_dime...  147 us
  transfers between devices with their start and end apart: 5, of which 5 were waited for; matrix products, arithmetic and copies ran while one was open for 3% of the time, Pallas kernels for 0%

profile of v1, /device:TPU:0, one launch (start us, length us, event | category | flops | bytes accessed | tf_op | source)
XLA Modules:
  0.0 1204.1 jit_solution(13717035341030003930)
XLA Ops:
  7.3 2.1 convolution_convert_fusion.10
  9.5 2.0 convolution_convert_fusion.9
  14.1 156.3 %all-gather.3.cloned.1.call-done = bf16[4096,512]{1,0:T(8,128)(2,1)} async-done(((bf16[128,512]{1,0:T(8,128)(2,1)}), bf16[4096,512]{1,0:T(8,128)(2,1)}) %all-gather.3.cloned.1.call-update) | async-done | bytes 4194320 | tf_op jit(solution)/shard_map/all_gather | solution.py:157
  170.4 1.9 fusion.99
  178.8 151.1 %all-gather.5.cloned.1.call-done = bf16[4096,512]{1,0:T(8,128)(2,1)} async-done(((bf16[128,512]{1,0:T(8,128)(2,1)}), bf16[4096,512]{1,0:T(8,128)(2,1)}) %all-gather.5.cloned.1.call-update) | async-done | bytes 4194320 | tf_op jit(solution)/shard_map/all_gather | solution.py:158
  329.9 2.7 convolution_convert_fusion.19
  343.8 3.6 maximum_convert_fusion.1
  348.1 2.7 multiply_reduce_fusion.3
  356.0 1.5 copy-done.4
  362.5 3.7 maximum_convert_fusion
  366.2 2.4 fusion.79
  368.6 1.9 convolution_convert_fusion.15
  370.6 1.8 convolution_convert_fusion.14
  373.7 1.4 fusion.78
  375.1 1.9 fusion.86
  377.0 1.8 fusion.55
  378.8 147.3 %reduce-scatter.5.cloned.1.call-done = f32[128,512]{1,0:T(8,128)} async-done(((f32[4096,512]{1,0:T(8,128)}), f32[128,512]{1,0:T(8,128)}) %reduce-scatter.5.cloned.1.call-update) | async-done | bytes 262160 | tf_op jit(solution)/shard_map/reduce_scatter | solution.py:175
  526.0 2.6 convolution_bitcast_fusion
  528.7 175.2 %reduce-scatter.3.cloned.1.call-done = f32[128,512]{1,0:T(8,128)} async-done(((f32[4096,512]{1,0:T(8,128)}), f32[128,512]{1,0:T(8,128)}) %reduce-scatter.3.cloned.1.call-update) | async-done | bytes 262160 | tf_op jit(solution)/shard_map/reduce_scatter | solution.py:174
  703.9 2.5 convolution_bitcast_fusion.1
  707.8 78.4 %all-reduce = (f32[512]{0:T(512)S(1)}, f32[512]{0:T(512)S(1)}) all-reduce(f32[512]{0:T(512)S(1)} %fusion.14, f32[512]{0:T(512)S(1)} %get-tuple-element.18), channel_id=1, replica_groups=mesh['room'=4,'geom'=32] {'geom'}, use_global_device_ids=true, to_apply=%region_33.34 | all-reduce | flops 1024 | bytes 8192 | tf_op jit(solution)/shard_map/psum | solution.py:16
  786.2 2.2 fusion.15
  788.5 259.0 %all-reduce.6.cloned.1.call-done = (f32[512,512]{1,0:T(8,128)}, f32[512,512]{0,1:T(8,128)}, f32[512,512]{0,1:T(8,128)}, f32[512,512]{1,0:T(8,128)}, f32[512,1024]{1,0:T(8,128)}, /*index=5*/f32[1024,512]{1,0:T(8,128)}) async-done(((f32[512,512]{1,0:T(8,128)}, f32[512,512]{0,1:T(8,128)}, f32[512,512]{0,1:T(8,128)}, f32[512,512]{1,0:T(8,128)}, f32[512,1024]{1,0:T(8,128)}, /*index=5*/f32[1024,512]{1,0:T(8,128)}), ...) | async-done | bytes 8388624 | tf_op jit(solution)/shard_map/psum | solution.py:16
  1047.5 148.1 %all-reduce.7 = (bf16[512,512]{1,0:T(8,128)(2,1)}, bf16[512,512]{0,1:T(8,128)(2,1)S(1)}, bf16[512,512]{0,1:T(8,128)(2,1)S(1)}, bf16[512,512]{1,0:T(8,128)(2,1)},...) all-reduce(f32[512,512]{1,0:T(8,128)} %get-tuple-element.23, ...), channel_id=1, replica_groups=mesh['room'=4,'geom'=32] {'room'}, use_global_device_ids=true, to_apply=%region_19.20 | all-reduce | flops 2098176 | bytes 12589056 | tf_op jit(solution)/shard_map/psum | solution.py:16
  (218 shorter events, 35.1 us)
Async XLA Ops:
  7.2 330.5 %copy-start = (bf16[512,1024]{1,0:T(8,128)(2,1)S(1)}, bf16[512,1024]{1,0:T(8,128)(2,1)}, u32[]{:S(2)}) copy-start(bf16[512,1024]{1,0:T(8,128)(2,1)} %param.20) | copy-start | bytes 3145732
  7.2 6.6 copy-start.19
  7.2 6.5 copy-start.80
  7.2 6.6 copy-start.29
  7.2 6.6 copy-start.44
  7.2 163.2 %all-gather.3.cloned.1.call-start = ((), (), s32[]{:S(2)}) async-start(), calls=%async_computation.2 | async-start | bytes 4325376 | tf_op jit(solution)/shard_map/all_gather | solution.py:157
  9.4 320.5 %all-gather.5.cloned.1.call-start = ((), (), s32[]{:S(2)}) async-start(), calls=%async_computation.3 | async-start | bytes 4325376 | tf_op jit(solution)/shard_map/all_gather | solution.py:158
  11.5 514.5 %reduce-scatter.5.cloned.1.call-start = ((), (), s32[]{:S(2)}) async-start(), calls=%async_computation.5 | async-start | bytes 8650752 | tf_op jit(solution)/shard_map/reduce_scatter | solution.py:175
  12.6 161.6 %copy-start.47 = (f32[128]{0:T(128)}, f32[128]{0:T(128)S(1)}, u32[]{:S(2)}) copy-start(f32[128]{0:T(128)S(1)} %broadcast_multiply_fusion.3) | copy-start | bytes 1540
  13.7 158.6 %copy-start.62 = (f32[128]{0:T(128)}, f32[128]{0:T(128)S(1)}, u32[]{:S(2)}) copy-start(f32[128]{0:T(128)S(1)} %add_rsqrt_fusion.1) | copy-start | bytes 1540
  14.1 163.4 %copy-start.24 = (bf16[128,512]{1,0:T(8,128)(2,1)}, bf16[128,512]{1,0:T(8,128)(2,1)S(1)}, u32[]{:S(2)}) copy-start(bf16[128,512]{1,0:T(8,128)(2,1)S(1)} %convolution_convert_fusion.11) | copy-start | bytes 393220
  172.3 157.6 %copy-start.58 = (f32[128]{0:T(128)}, f32[128]{0:T(128)S(1)}, u32[]{:S(2)}) copy-start(f32[128]{0:T(128)S(1)} %get-tuple-element.43) | copy-start | bytes 1540
  174.1 155.8 %copy-start.73 = (f32[128]{0:T(128)}, f32[128]{0:T(128)S(1)}, u32[]{:S(2)}) copy-start(f32[128]{0:T(128)S(1)} %fusion.5) | copy-start | bytes 1540
  174.7 157.9 %copy-start.55 = (f32[128]{0:T(128)}, f32[128]{0:T(128)S(1)}, u32[]{:S(2)}) copy-start(f32[128]{0:T(128)S(1)} %get-tuple-element.41) | copy-start | bytes 1540
  176.4 156.2 %copy-start.70 = (f32[128]{0:T(128)}, f32[128]{0:T(128)S(1)}, u32[]{:S(2)}) copy-start(f32[128]{0:T(128)S(1)} %fusion.7) | copy-start | bytes 1540
  177.0 157.4 %copy-start.52 = (f32[128]{0:T(128)}, f32[128]{0:T(128)S(1)}, u32[]{:S(2)}) copy-start(f32[128]{0:T(128)S(1)} %get-tuple-element.39) | copy-start | bytes 1540
  177.5 157.0 %copy-start.67 = (f32[128]{0:T(128)}, f32[128]{0:T(128)S(1)}, u32[]{:S(2)}) copy-start(f32[128]{0:T(128)S(1)} %fusion.9) | copy-start | bytes 1540
  178.3 157.7 %copy-start.49 = (f32[128]{0:T(128)}, f32[128]{0:T(128)S(1)}, u32[]{:S(2)}) copy-start(f32[128]{0:T(128)S(1)} %get-tuple-element.37) | copy-start | bytes 1540
  178.8 157.3 %copy-start.64 = (f32[128]{0:T(128)}, f32[128]{0:T(128)S(1)}, u32[]{:S(2)}) copy-start(f32[128]{0:T(128)S(1)} %fusion.11) | copy-start | bytes 1540
  347.4 356.4 %reduce-scatter.3.cloned.1.call-start = ((), (), s32[]{:S(2)}) async-start(), calls=%async_computation.4 | async-start | bytes 8650752 | tf_op jit(solution)/shard_map/reduce_scatter | solution.py:174
  366.1 6.3 copy-start.16
  366.2 681.3 %all-reduce.6.cloned.1.call-start = ((), (), s32[]{:S(2)}) async-start(), calls=%async_computation.6 | async-start | bytes 16777216 | tf_op jit(solution)/shard_map/psum | solution.py:16
  375.1 151.0 %copy-start.23 = (bf16[1,128,512]{2,1,0:T(8,128)(2,1)S(1)}, bf16[1,128,512]{2,1,0:T(8,128)(2,1)}, u32[]{:S(2)}) copy-start(bf16[1,128,512]{2,1,0:T(8,128)(2,1)} %param.13) | copy-start | bytes 393220
  1047.5 150.1 %copy-start.1 = (bf16[512,1024]{1,0:T(8,128)(2,1)S(1)}, bf16[512,1024]{1,0:T(8,128)(2,1)}, u32[]{:S(2)}) copy-start(bf16[512,1024]{1,0:T(8,128)(2,1)} %param.20) | copy-start | bytes 3145732
  (62 other events, 110.7 us)
Sparse Core Ops, SparseCore 0:
  10.3 160.0 all-gather.2
  172.6 157.2 all-gather.4
  347.6 178.4 reduce-scatter.4
  528.3 175.5 reduce-scatter.2
  707.3 340.1 all-reduce.5
